TPU v7x, 32 devices: a whole 2x2x4 slice. The times are simulated.
32 devices in a mesh: wide: 8 (over z, x), narrow: 4 (over y, core).
Axes of the slice: x: 2, y: 2, z: 4, core: 2. Of those that a mesh axis runs over, the one named last changes fastest.
Arguments:
- flow_field: bfloat16 [64, 64, 16, 512], P('wide', 'narrow'), may hold values from -48 to 48
- fluid_mask: int32 [64, 64, 16], P('wide', 'narrow'), may hold values 0 or 1
- conv_weight: float32 [27, 512], replicated, may hold values from -1 to 1
- latents: bfloat16 [1024, 512], replicated, may hold values from -6 to 6
- w_query1: bfloat16 [512, 512], replicated, may hold values from -0.25 to 0.25
- w_key1: bfloat16 [512, 512], replicated, may hold values from -0.25 to 0.25
- w_value1: bfloat16 [512, 512], replicated, may hold values from -0.25 to 0.25
- w_out1: bfloat16 [512, 512], replicated, may hold values from -0.25 to 0.25
- w_query2: bfloat16 [512, 512], replicated, may hold values from -0.25 to 0.25
- w_key2: bfloat16 [512, 512], replicated, may hold values from -0.25 to 0.25
- w_value2: bfloat16 [512, 512], replicated, may hold values from -0.25 to 0.25
- w_out2: bfloat16 [512, 512], replicated, may hold values from -0.25 to 0.25
Outputs:
- updated_field: float32 [64, 64, 16, 512], P('wide', 'narrow')
All inputs are finite; a program needn't handle non-finite values. No bound on the sum of `fluid_mask` on one device may be relied on, other than what follows from the above.
Results may differ from a plain program's by a relative error of at most 0.035.
The roundings to bfloat16 on the way count: a program that leaves them out, or rounds other values in their place, can miss the bound.
Values may be sent and summed in bfloat16 or wider, within the bound.
No kernel may reach another device: no remote copies, remote signals or barrier semaphores. Data moves between devices by JAX's collectives and lax.ppermute only.
A program may use at most 192 MiB of HBM per device.

v0:
```python
import math
import jax
import jax.numpy as jnp
from jax import lax
from jax.sharding import PartitionSpec as P

HEADS = 8


def padded_2(cells, sides, width):
    for axis, dim in sides:
        count = lax.axis_size(axis)
        ends = count - 1
        head = lax.slice_in_dim(cells, 0, width, axis=dim)
        tail = lax.slice_in_dim(cells, cells.shape[dim] - width, cells.shape[dim], axis=dim)
        cells = jnp.concatenate(
            [
                lax.ppermute(tail, axis, [(i, (i + 1) % count) for i in range(ends)]),
                cells,
                lax.ppermute(head, axis, [((i + 1) % count, i) for i in range(ends)]),
            ],
            axis=dim,
        )
    return cells


def head_block(matrix, head_index, head_size):
    return matrix[:, head_index * head_size : (head_index + 1) * head_size]


def pair_scores(queries, key_rows, head_size):
    factor = 1.8 / math.sqrt(head_size)
    return factor * lax.dot_general(
        queries, key_rows, (((1,), (1,)), ((), ())), preferred_element_type=jnp.float32
    )


def project(row_block, weight):
    return jnp.dot(row_block, weight, preferred_element_type=jnp.float32).astype(jnp.bfloat16)


def exact_dot(weights, values_block):
    return jnp.dot(
        weights, values_block, precision=lax.Precision.HIGHEST, preferred_element_type=jnp.float32
    )


def update_state(summed, totals, state_rows, w_out1, head_count):
    row_count, model_width = summed.shape
    shaped = summed.reshape(row_count, head_count, model_width // head_count) / totals[:, :, None]
    read_rows = shaped.reshape(row_count, model_width).astype(jnp.bfloat16)
    updated = state_rows.astype(jnp.float32) + jnp.dot(
        read_rows, w_out1, preferred_element_type=jnp.float32
    )
    return updated.astype(jnp.bfloat16)


def per_device(
    flow_field,
    fluid_mask,
    conv_weight,
    latents,
    w_query1,
    w_key1,
    w_value1,
    w_out1,
    w_query2,
    w_key2,
    w_value2,
    w_out2,
):
    size_x, size_y, size_z, model_width = flow_field.shape
    head_count = HEADS
    head_size = model_width // head_count
    latent_count = latents.shape[0]
    masked = flow_field * fluid_mask[:, :, :, None].astype(jnp.bfloat16)
    padded = padded_2(masked, (("wide", 0), ("narrow", 1)), 1)
    padded = jnp.pad(padded, ((0, 0), (0, 0), (1, 1), (0, 0)))
    stencil = masked.astype(jnp.float32)
    for offset_x in range(3):
        for offset_y in range(3):
            for offset_z in range(3):
                window = padded[
                    offset_x : offset_x + size_x,
                    offset_y : offset_y + size_y,
                    offset_z : offset_z + size_z,
                ]
                stencil = (
                    stencil
                    + window.astype(jnp.float32)
                    * conv_weight[9 * offset_x + 3 * offset_y + offset_z]
                )
    cell_count = size_x * size_y * size_z
    mixed_cells = stencil.astype(jnp.bfloat16).reshape(cell_count, model_width)
    flat_masked = masked.reshape(cell_count, model_width)
    keys1 = project(mixed_cells, w_key1)
    values1 = project(mixed_cells, w_value1)
    values_wide = values1.astype(jnp.float32)
    queries1 = project(latents, w_query1)
    device_count = lax.axis_size("wide") * lax.axis_size("narrow")
    sums_list = []
    totals_list = []
    tops_list = []
    for head_index in range(head_count):
        scores = pair_scores(
            head_block(queries1, head_index, head_size),
            head_block(keys1, head_index, head_size),
            head_size,
        )
        own_top = jnp.max(scores, axis=1, keepdims=True)
        weights = jnp.exp(scores - own_top)
        tops_list.append(own_top[:, 0])
        totals_list.append(jnp.sum(weights, axis=1))
        sums_list.append(exact_dot(weights, head_block(values_wide, head_index, head_size)))
    summed1 = jnp.concatenate(sums_list, axis=1)[None]
    totals1 = jnp.stack(totals_list, axis=1)[None]
    tops1 = jnp.stack(tops_list, axis=1)[None]
    part_sums, part_totals, part_tops = (
        lax.all_to_all(summed1, ("wide", "narrow"), split_axis=1, concat_axis=0, tiled=True),
        lax.all_to_all(totals1, ("wide", "narrow"), split_axis=1, concat_axis=0, tiled=True),
        lax.all_to_all(tops1, ("wide", "narrow"), split_axis=1, concat_axis=0, tiled=True),
    )
    row_count = latent_count // device_count
    largest = jnp.max(part_tops, axis=0, keepdims=True)
    factors = jnp.exp(part_tops - largest)
    totals = jnp.sum(factors * part_totals, axis=0)
    shaped = (
        part_sums.reshape(device_count, row_count, head_count, head_size) * factors[:, :, :, None]
    )
    summed = jnp.sum(shaped, axis=0).reshape(row_count, model_width)
    start = (
        lax.axis_index("wide") * lax.axis_size("narrow") + lax.axis_index("narrow")
    ) * row_count
    own_latents = lax.dynamic_slice_in_dim(latents, start, row_count, 0)
    own_state = update_state(summed, totals, own_latents, w_out1, head_count)
    latent_state = lax.all_gather(own_state, ("wide", "narrow"), axis=0, tiled=True)
    keys2 = project(latent_state, w_key2)
    values2 = project(latent_state, w_value2)
    queries2 = project(mixed_cells, w_query2)
    read_heads = []
    for head_index in range(head_count):
        scores = pair_scores(
            head_block(queries2, head_index, head_size),
            head_block(keys2, head_index, head_size),
            head_size,
        )
        top2 = jnp.max(scores, axis=1, keepdims=True)
        weights = jnp.exp(scores - top2)
        totals = jnp.sum(weights, axis=1, keepdims=True)
        summed = jnp.dot(
            weights.astype(jnp.bfloat16),
            head_block(values2, head_index, head_size),
            preferred_element_type=jnp.float32,
        )
        read_heads.append(summed / totals)
    read2 = jnp.concatenate(read_heads, axis=1).astype(jnp.bfloat16)
    result = flat_masked.astype(jnp.float32) + jnp.dot(
        read2, w_out2, preferred_element_type=jnp.float32
    )
    return result.reshape(size_x, size_y, size_z, model_width)


def solution(mesh):
    return jax.shard_map(
        per_device,
        mesh=mesh,
        in_specs=(
            P("wide", "narrow", None, None),
            P("wide", "narrow", None),
            P(),
            P(),
            P(),
            P(),
            P(),
            P(),
            P(),
            P(),
            P(),
            P(),
        ),
        out_specs=P("wide", "narrow", None, None),
        check_vma=False,
    )
```

profile of v0, /device:TPU:0, one launch (start us, length us, event | category | flops | bytes accessed | tf_op | source)
XLA Modules:
  0.0 399.7 jit_solution(2876258442550393296)
XLA Ops:
  7.5 1.9 broadcast_multiply_fusion
  9.5 4.9 %collective-permute-start = (bf16[1,16,16,512]{3,2,1,0:T(8,128)(2,1)S(1)}, bf16[1,16,16,512]{3,2,1,0:T(8,128)(2,1)S(1)}, u32[]{:S(2)}, u32[]{:S(2)}) collective-permute-start(bf16[1,16,16,512]{3,2,1,0:T(8,128)(2,1)S(1)} %get-tuple-element.11), channel_id=1, source_target_pairs={{0,4},{4,8},{8,12},{12,16},{16,20},{20,24},{24,28},{1,5},{5,9},{9,... | collective-permute-start | bytes 786440 | tf_op jit(solution)/shard_map/ppermute | solution.py:18
  16.6 9.0 %collective-permute-done = bf16[1,16,16,512]{3,2,1,0:T(8,128)(2,1)S(1)} collective-permute-done((bf16[1,16,16,512]{3,2,1,0:T(8,128)(2,1)S(1)}, bf16[1,16,16,512]{3,2,1,0:T(8,128)(2,1)S(1)}, u32[]{:S(2)}, u32[]{:S(2)}) %collective-permute-start) | collective-permute-done | bytes 262176 | tf_op jit(solution)/shard_map/ppermute | solution.py:18
  28.3 3.7 collective-permute-done.3
  32.0 2.8 select_maximum_fusion
  35.7 16.4 %add_convert_fusion = bf16[8,16,16,512]{3,2,1,0:T(8,128)(2,1)S(1)} fusion(bf16[8,16,16,512]{3,2,1,0:T(8,128)(2,1)S(1)} %broadcast_multiply_fusion, bf16[10,18,18,512]{3,2,1,0:T(8,128)(2,1)S(1)} %select_maximum_fusion, bf16[10,17,16,512]{3,2,1,0:T(8,128)(2,1)S(1)} %get-tuple-element.8, bf16[1,16,16,512]{3,2,1,0:T(8,128)(2,1)S(1)} %collective-permute-done.1, ...), kind=kLoop, calls=%fused_computation.91 | loop fusion | flops 88080384 | bytes 55105536 | tf_op jit(solution)/shard_map/convert_element_type | solution.py:94
  57.5 1.4 multiply_reduce_fusion.11
  58.8 4.5 %multiply_reduce_fusion.12 = (f32[1024]{0:T(1024)S(1)}, f32[1024,2048]{1,0:T(8,128)}) fusion(bf16[2048,512]{0,1:T(8,128)(2,1)S(1)} %convolution_convert_fusion.1, bf16[1024,512]{0,1:T(8,128)(2,1)S(1)} %convolution_convert_fusion.5), kind=kOutput, calls=%fused_computation.31 | convolution fusion | flops 272628736 | bytes 8785920 | tf_op jit(solution)/shard_map/dot_general | solution.py:33
  63.3 4.5 %multiply_reduce_fusion.13 = (f32[1024]{0:T(1024)S(1)}, f32[1024,2048]{1,0:T(8,128)}) fusion(bf16[2048,512]{0,1:T(8,128)(2,1)S(1)} %convolution_convert_fusion.1, bf16[1024,512]{0,1:T(8,128)(2,1)S(1)} %convolution_convert_fusion.5), kind=kOutput, calls=%fused_computation.32 | convolution fusion | flops 272628736 | bytes 8785920 | tf_op jit(solution)/shard_map/dot_general | solution.py:33
  67.8 4.5 %multiply_reduce_fusion.14 = (f32[1024]{0:T(1024)S(1)}, f32[1024,2048]{1,0:T(8,128)}) fusion(bf16[2048,512]{0,1:T(8,128)(2,1)S(1)} %convolution_convert_fusion.1, bf16[1024,512]{0,1:T(8,128)(2,1)S(1)} %convolution_convert_fusion.5), kind=kOutput, calls=%fused_computation.33 | convolution fusion | flops 272628736 | bytes 8785920 | tf_op jit(solution)/shard_map/dot_general | solution.py:33
  72.3 4.5 %multiply_reduce_fusion.15 = (f32[1024]{0:T(1024)S(1)}, f32[1024,2048]{1,0:T(8,128)}) fusion(bf16[2048,512]{0,1:T(8,128)(2,1)S(1)} %convolution_convert_fusion.1, bf16[1024,512]{0,1:T(8,128)(2,1)S(1)} %convolution_convert_fusion.5), kind=kOutput, calls=%fused_computation.34 | convolution fusion | flops 272628736 | bytes 8785920 | tf_op jit(solution)/shard_map/dot_general | solution.py:33
  76.8 2.8 convolution_convert_fusion
  79.6 4.4 %fusion.1 = f32[1024]{0:T(1024)S(1)} fusion(f32[1024,2048]{1,0:T(8,128)} %get-tuple-element.41, f32[1024]{0:T(1024)S(1)} %get-tuple-element.40), kind=kLoop, calls=%fused_computation.35 | loop fusion | flops 6290432 | bytes 8396800 | tf_op jit(solution)/shard_map/reduce_sum | solution.py:113
  83.9 7.9 %fusion.149 = f32[1024,512]{0,1:T(8,128)S(1)} fusion(f32[1024,2048]{1,0:T(8,128)} %get-tuple-element.41, f32[1024]{0:T(1024)S(1)} %get-tuple-element.40, bf16[2048,512]{0,1:T(8,128)(2,1)} %convolution_convert_fusion), kind=kOutput, calls=%fused_computation.142 | convolution fusion | flops 1614807040 | bytes 8916992 | tf_op jit(solution)/shard_map/dot_general | solution.py:43
  91.8 4.4 %fusion.3 = f32[1024]{0:T(1024)S(1)} fusion(f32[1024,2048]{1,0:T(8,128)} %get-tuple-element.43, f32[1024]{0:T(1024)S(1)} %get-tuple-element.42), kind=kLoop, calls=%fused_computation.37 | loop fusion | flops 6290432 | bytes 8396800 | tf_op jit(solution)/shard_map/reduce_sum | solution.py:113
  96.2 8.1 %fusion.148 = f32[1024,512]{0,1:T(8,128)S(1)} fusion(f32[1024,512]{0,1:T(8,128)S(1)} %fusion.149, f32[1024,2048]{1,0:T(8,128)} %get-tuple-element.43, f32[1024]{0:T(1024)S(1)} %get-tuple-element.42, bf16[2048,512]{0,1:T(8,128)(2,1)} %convolution_convert_fusion), kind=kOutput, calls=%fused_computation.141 | convolution fusion | flops 1614807040 | bytes 8916992 | tf_op jit(solution)/shard_map/dot_general | solution.py:43
  104.3 4.4 %fusion.5 = f32[1024]{0:T(1024)S(1)} fusion(f32[1024,2048]{1,0:T(8,128)} %get-tuple-element.45, f32[1024]{0:T(1024)S(1)} %get-tuple-element.44), kind=kLoop, calls=%fused_computation.39 | loop fusion | flops 6290432 | bytes 8396800 | tf_op jit(solution)/shard_map/reduce_sum | solution.py:113
  108.7 8.1 %fusion.147 = f32[1024,512]{0,1:T(8,128)S(1)} fusion(f32[1024,512]{0,1:T(8,128)S(1)} %fusion.148, f32[1024,2048]{1,0:T(8,128)} %get-tuple-element.45, f32[1024]{0:T(1024)S(1)} %get-tuple-element.44, bf16[2048,512]{0,1:T(8,128)(2,1)} %convolution_convert_fusion), kind=kOutput, calls=%fused_computation.140 | convolution fusion | flops 1614807040 | bytes 8916992 | tf_op jit(solution)/shard_map/dot_general | solution.py:43
  116.8 4.4 %fusion.7 = f32[1024]{0:T(1024)S(1)} fusion(f32[1024,2048]{1,0:T(8,128)} %get-tuple-element.47, f32[1024]{0:T(1024)S(1)} %get-tuple-element.46), kind=kLoop, calls=%fused_computation.41 | loop fusion | flops 6290432 | bytes 8396800 | tf_op jit(solution)/shard_map/reduce_sum | solution.py:113
  121.1 8.3 %fusion.146 = f32[1024,512]{0,1:T(8,128)S(1)} fusion(f32[1024,512]{0,1:T(8,128)S(1)} %fusion.147, f32[1024,2048]{1,0:T(8,128)} %get-tuple-element.47, f32[1024]{0:T(1024)S(1)} %get-tuple-element.46, bf16[2048,512]{0,1:T(8,128)(2,1)} %convolution_convert_fusion), kind=kOutput, calls=%fused_computation.139 | convolution fusion | flops 1614807040 | bytes 8916992 | tf_op jit(solution)/shard_map/dot_general | solution.py:43
  129.5 1.9 fusion.9
  131.4 6.5 %fusion.145 = f32[1024,512]{0,1:T(8,128)S(1)} fusion(f32[1024,512]{0,1:T(8,128)S(1)} %fusion.146, f32[1024,2048]{1,0:T(8,128)S(1)} %get-tuple-element.49, f32[1024]{0:T(1024)S(1)} %get-tuple-element.48, bf16[2048,512]{0,1:T(8,128)(2,1)} %convolution_convert_fusion), kind=kOutput, calls=%fused_computation.138 | convolution fusion | flops 1614807040 | bytes 8916992 | tf_op jit(solution)/shard_map/dot_general | solution.py:43
  137.9 2.3 fusion.11
  140.2 6.5 %fusion.144 = f32[1024,512]{0,1:T(8,128)S(1)} fusion(f32[1024,512]{0,1:T(8,128)S(1)} %fusion.145, f32[1024,2048]{1,0:T(8,128)S(1)} %get-tuple-element.51, f32[1024]{0:T(1024)S(1)} %get-tuple-element.50, bf16[2048,512]{0,1:T(8,128)(2,1)} %convolution_convert_fusion), kind=kOutput, calls=%fused_computation.137 | convolution fusion | flops 1614807040 | bytes 8916992 | tf_op jit(solution)/shard_map/dot_general | solution.py:43
  146.7 1.9 fusion.15
  148.6 1.9 fusion.13
  151.5 1.9 reduce.3
  154.3 9.5 %all-to-all-start.1 = ((f32[32,1,256]{2,1,0:T(1,128)}), f32[32,1,256]{2,1,0:T(1,128)S(1)}, u32[]{:S(2)}, u32[]{:S(2)}) async-start(f32[32,1,256]{2,1,0:T(1,128)} %reshape.112), calls=%async_computation.1 | async-start | bytes 65536 | tf_op jit(solution)/shard_map/all_to_all | solution.py:121
  163.8 8.1 %fusion.143 = f32[1024,512]{0,1:T(8,128)S(1)} fusion(f32[1024,512]{0,1:T(8,128)S(1)} %fusion.144, f32[1024,2048]{1,0:T(8,128)} %copy-done.3, f32[1024]{0:T(1024)S(1)} %get-tuple-element.52, bf16[2048,512]{0,1:T(8,128)(2,1)} %convolution_convert_fusion), kind=kOutput, calls=%fused_computation.136 | convolution fusion | flops 1614807040 | bytes 8916992 | tf_op jit(solution)/shard_map/dot_general | solution.py:43
  172.3 1.9 reduce.1
  175.1 5.9 %all-to-all-start.2 = ((f32[32,1,256]{2,1,0:T(1,128)}), f32[32,1,256]{2,1,0:T(1,128)S(1)}, u32[]{:S(2)}, u32[]{:S(2)}) async-start(f32[32,1,256]{2,1,0:T(1,128)} %reshape.114), calls=%async_computation.2 | async-start | bytes 65536 | tf_op jit(solution)/shard_map/all_to_all | solution.py:120
  181.1 8.1 %fusion.142 = f32[1024,512]{0,1:T(8,128)S(1)} fusion(f32[1024,512]{0,1:T(8,128)S(1)} %fusion.143, f32[1024,2048]{1,0:T(8,128)} %copy-done.2, f32[1024]{0:T(1024)S(1)} %get-tuple-element.54, bf16[2048,512]{0,1:T(8,128)(2,1)} %convolution_convert_fusion), kind=kOutput, calls=%fused_computation.135 | convolution fusion | flops 1614807040 | bytes 8916992 | tf_op jit(solution)/shard_map/dot_general | solution.py:43
  189.2 3.7 copy.23
  192.9 6.0 %all-to-all-start = ((f32[1,1024,512]{2,0,1:T(1,128)}), f32[1,1024,512]{2,0,1:T(1,128)}, u32[]{:S(2)}, u32[]{:S(2)}) async-start(f32[1,1024,512]{2,0,1:T(1,128)} %copy.23), calls=%async_computation | async-start | bytes 4194304 | tf_op jit(solution)/shard_map/all_to_all | solution.py:119
  203.2 2.6 mul.451
  205.8 3.6 mul.452
  209.5 38.1 %all-to-all-done = f32[1,1024,512]{2,0,1:T(1,128)} async-done(((f32[1,1024,512]{2,0,1:T(1,128)}), f32[1,1024,512]{2,0,1:T(1,128)}, u32[]{:S(2)}, u32[]{:S(2)}) %all-to-all-start) | async-done | bytes 2097184 | tf_op jit(solution)/shard_map/all_to_all | solution.py:119
  247.6 1.8 copy.31
  249.8 1.6 fusion.150
  251.4 2.9 convolution_convert_fusion.2
  254.4 50.3 %all-gather.2.cloned.1.call-done = bf16[1024,512]{1,0:T(8,128)(2,1)} async-done(((bf16[32,512]{1,0:T(8,128)(2,1)}), bf16[1024,512]{1,0:T(8,128)(2,1)}) %all-gather.2.cloned.1.call-update) | async-done | bytes 1048592 | tf_op jit(solution)/shard_map/all_gather | solution.py:136
  304.7 2.0 convolution_convert_fusion.4
  310.6 4.5 %multiply_reduce_fusion.3 = (f32[2048]{0:T(1024)S(1)}, f32[2048,1024]{0,1:T(8,128)}) fusion(bf16[1024,512]{0,1:T(8,128)(2,1)S(1)} %convolution_convert_fusion.4, bf16[2048,512]{0,1:T(8,128)(2,1)S(1)} %convolution_convert_fusion.2), kind=kOutput, calls=%fused_computation.22 | convolution fusion | flops 272627712 | bytes 8790016 | tf_op jit(solution)/shard_map/dot_general | solution.py:33
  315.1 4.5 %multiply_reduce_fusion.4 = (f32[2048]{0:T(1024)S(1)}, f32[2048,1024]{0,1:T(8,128)}) fusion(bf16[1024,512]{0,1:T(8,128)(2,1)S(1)} %convolution_convert_fusion.4, bf16[2048,512]{0,1:T(8,128)(2,1)S(1)} %convolution_convert_fusion.2), kind=kOutput, calls=%fused_computation.23 | convolution fusion | flops 272627712 | bytes 8790016 | tf_op jit(solution)/shard_map/dot_general | solution.py:33
  319.6 4.5 %multiply_reduce_fusion.5 = (f32[2048]{0:T(1024)S(1)}, f32[2048,1024]{0,1:T(8,128)}) fusion(bf16[1024,512]{0,1:T(8,128)(2,1)S(1)} %convolution_convert_fusion.4, bf16[2048,512]{0,1:T(8,128)(2,1)S(1)} %convolution_convert_fusion.2), kind=kOutput, calls=%fused_computation.24 | convolution fusion | flops 272627712 | bytes 8790016 | tf_op jit(solution)/shard_map/dot_general | solution.py:33
  324.2 4.5 %multiply_reduce_fusion.6 = (f32[2048]{0:T(1024)S(1)}, f32[2048,1024]{0,1:T(8,128)}) fusion(bf16[1024,512]{0,1:T(8,128)(2,1)S(1)} %convolution_convert_fusion.4, bf16[2048,512]{0,1:T(8,128)(2,1)S(1)} %convolution_convert_fusion.2), kind=kOutput, calls=%fused_computation.25 | convolution fusion | flops 272627712 | bytes 8790016 | tf_op jit(solution)/shard_map/dot_general | solution.py:33
  328.7 5.0 %multiply_reduce_fusion.7 = (f32[2048]{0:T(1024)S(1)}, f32[2048,1024]{0,1:T(8,128)}) fusion(bf16[1024,512]{0,1:T(8,128)(2,1)S(1)} %convolution_convert_fusion.4, bf16[2048,512]{0,1:T(8,128)(2,1)S(1)} %convolution_convert_fusion.2), kind=kOutput, calls=%fused_computation.26 | convolution fusion | flops 272627712 | bytes 8790016 | tf_op jit(solution)/shard_map/dot_general | solution.py:33
  333.7 1.4 fusion.31
  335.1 1.4 fusion.29
  336.5 1.4 fusion.27
  337.9 4.8 %fusion.25 = f32[2048]{0:T(1024)S(1)} fusion(f32[2048,1024]{0,1:T(8,128)} %get-tuple-element.65, f32[2048]{0:T(1024)S(1)} %get-tuple-element.64), kind=kLoop, calls=%fused_computation.59 | loop fusion | flops 6289408 | bytes 8404992 | tf_op jit(solution)/shard_map/reduce_sum | solution.py:149
  342.7 4.8 %fusion.23 = f32[2048]{0:T(1024)S(1)} fusion(f32[2048,1024]{0,1:T(8,128)} %get-tuple-element.63, f32[2048]{0:T(1024)S(1)} %get-tuple-element.62), kind=kLoop, calls=%fused_computation.57 | loop fusion | flops 6289408 | bytes 8404992 | tf_op jit(solution)/shard_map/reduce_sum | solution.py:149
  347.4 4.8 %fusion.21 = f32[2048]{0:T(1024)S(1)} fusion(f32[2048,1024]{0,1:T(8,128)} %get-tuple-element.61, f32[2048]{0:T(1024)S(1)} %get-tuple-element.60), kind=kLoop, calls=%fused_computation.55 | loop fusion | flops 6289408 | bytes 8404992 | tf_op jit(solution)/shard_map/reduce_sum | solution.py:149
  352.2 4.8 %fusion.19 = f32[2048]{0:T(1024)S(1)} fusion(f32[2048,1024]{0,1:T(8,128)} %get-tuple-element.59, f32[2048]{0:T(1024)S(1)} %get-tuple-element.58), kind=kLoop, calls=%fused_computation.53 | loop fusion | flops 6289408 | bytes 8404992 | tf_op jit(solution)/shard_map/reduce_sum | solution.py:149
  357.0 5.1 %fusion.17 = f32[2048]{0:T(1024)S(1)} fusion(f32[2048,1024]{0,1:T(8,128)} %get-tuple-element.57, f32[2048]{0:T(1024)S(1)} %get-tuple-element.56), kind=kLoop, calls=%fused_computation.51 | loop fusion | flops 6289408 | bytes 8404992 | tf_op jit(solution)/shard_map/reduce_sum | solution.py:149
  362.9 4.9 %fusion.76 = bf16[2048,512]{0,1:T(8,128)(2,1)S(1)} fusion(f32[2048,1024]{0,1:T(8,128)} %get-tuple-element.57, f32[2048]{0:T(1024)S(1)} %get-tuple-element.56, f32[2048]{0:T(1024)S(1)} %fusion.17, bf16[1024,512]{0,1:T(8,128)(2,1)S(1)} %convolution_convert_fusion.3), kind=kOutput, calls=%fused_computation.107 | convolution fusion | flops 274989056 | bytes 8798208 | tf_op jit(solution)/shard_map/dot_general | solution.py:150
  367.8 4.9 %fusion.85 = bf16[2048,512]{0,1:T(8,128)(2,1)S(1)} fusion(bf16[2048,512]{0,1:T(8,128)(2,1)S(1)} %fusion.76, f32[2048,1024]{0,1:T(8,128)} %get-tuple-element.59, f32[2048]{0:T(1024)S(1)} %get-tuple-element.58, f32[2048]{0:T(1024)S(1)} %fusion.19, bf16[1024,512]{0,1:T(8,128)(2,1)S(1)} %convolution_convert_fusion.3), kind=kOutput, calls=%fused_computation.110 | convolution fusion | flops 274989056 | bytes 8798208 | tf_op jit(solution)/shard_map/dot_general | solution.py:150
  372.8 5.1 %fusion.94 = bf16[2048,512]{0,1:T(8,128)(2,1)S(1)} fusion(bf16[2048,512]{0,1:T(8,128)(2,1)S(1)} %fusion.85, f32[2048,1024]{0,1:T(8,128)} %get-tuple-element.61, f32[2048]{0:T(1024)S(1)} %get-tuple-element.60, f32[2048]{0:T(1024)S(1)} %fusion.21, bf16[1024,512]{0,1:T(8,128)(2,1)S(1)} %convolution_convert_fusion.3), kind=kOutput, calls=%fused_computation.113 | convolution fusion | flops 274989056 | bytes 8798208 | tf_op jit(solution)/shard_map/dot_general | solution.py:150
  377.8 5.1 %fusion.103 = bf16[2048,512]{0,1:T(8,128)(2,1)S(1)} fusion(bf16[2048,512]{0,1:T(8,128)(2,1)S(1)} %fusion.94, f32[2048,1024]{0,1:T(8,128)} %get-tuple-element.63, f32[2048]{0:T(1024)S(1)} %get-tuple-element.62, f32[2048]{0:T(1024)S(1)} %fusion.23, bf16[1024,512]{0,1:T(8,128)(2,1)S(1)} %convolution_convert_fusion.3), kind=kOutput, calls=%fused_computation.116 | convolution fusion | flops 274989056 | bytes 8798208 | tf_op jit(solution)/shard_map/dot_general | solution.py:150
  382.9 1.6 fusion.112
  384.5 1.6 fusion.121
  386.1 1.6 fusion.130
  387.7 1.6 fusion.139
  389.3 3.3 bitcast_add_fusion
  (84 shorter events, 24.7 us)
Async XLA Ops:
  6.5 45.5 %copy-start = (bf16[512,512]{1,0:T(8,128)(2,1)S(1)}, bf16[512,512]{1,0:T(8,128)(2,1)}, u32[]{:S(2)}) copy-start(bf16[512,512]{1,0:T(8,128)(2,1)} %param.17) | copy-start | bytes 1572868
  6.5 9.2 %copy-start.9 = (f32[27,512]{1,0:T(8,128)S(1)}, f32[27,512]{1,0:T(8,128)}, u32[]{:S(2)}) copy-start(f32[27,512]{1,0:T(8,128)} %param.14) | copy-start | bytes 165892
  6.5 9.2 %copy-start.10 = (bf16[1024,512]{1,0:T(8,128)(2,1)S(1)}, bf16[1024,512]{1,0:T(8,128)(2,1)}, u32[]{:S(2)}) copy-start(bf16[1024,512]{1,0:T(8,128)(2,1)} %param.15) | copy-start | bytes 3145732
  6.5 9.2 %copy-start.12 = (bf16[512,512]{1,0:T(8,128)(2,1)S(1)}, bf16[512,512]{1,0:T(8,128)(2,1)}, u32[]{:S(2)}) copy-start(bf16[512,512]{1,0:T(8,128)(2,1)} %param.16) | copy-start | bytes 1572868
  9.5 26.2 %copy-start.4 = (bf16[8,16,16,512]{3,2,1,0:T(8,128)(2,1)}, bf16[8,16,16,512]{3,2,1,0:T(8,128)(2,1)S(1)}, u32[]{:S(2)}) copy-start(bf16[8,16,16,512]{3,2,1,0:T(8,128)(2,1)S(1)} %broadcast_multiply_fusion) | copy-start | bytes 6291460
  9.5 16.0 %collective-permute-start = (bf16[1,16,16,512]{3,2,1,0:T(8,128)(2,1)S(1)}, bf16[1,16,16,512]{3,2,1,0:T(8,128)(2,1)S(1)}, u32[]{:S(2)}, u32[]{:S(2)}) collective-permute-start(bf16[1,16,16,512]{3,2,1,0:T(8,128)(2,1)S(1)} %get-tuple-element.11), channel_id=1, source_target_pairs={{0,4},{4,8},{8,12},{12,16},{16,20},{20,24},{24,28},{1,5},{5,9},{9,... | collective-permute-start | bytes 786440 | tf_op jit(solution)/shard_map/ppermute | solution.py:18
  14.4 11.2 %collective-permute-start.1 = (bf16[1,16,16,512]{3,2,1,0:T(8,128)(2,1)S(1)}, bf16[1,16,16,512]{3,2,1,0:T(8,128)(2,1)S(1)}, u32[]{:S(2)}, u32[]{:S(2)}) collective-permute-start(bf16[1,16,16,512]{3,2,1,0:T(8,128)(2,1)S(1)} %get-tuple-element.12), channel_id=1, source_target_pairs={{4,0},{8,4},{12,8},{16,12},{20,16},{24,20},{28,24},{5,1},{9,5},{13... | collective-permute-start | bytes 786440 | tf_op jit(solution)/shard_map/ppermute | solution.py:20
  25.6 2.6 collective-permute-start.2
  26.9 5.0 %collective-permute-start.3 = (bf16[10,1,16,512]{3,2,1,0:T(8,128)(2,1)S(1)}, bf16[10,1,16,512]{3,2,1,0:T(8,128)(2,1)S(1)}, u32[]{:S(2)}, u32[]{:S(2)}) collective-permute-start(bf16[10,1,16,512]{3,2,1,0:T(8,128)(2,1)S(1)} %get-tuple-element.10), channel_id=1, source_target_pairs={{1,0},{2,1},{3,2},{5,4},{6,5},{7,6},{9,8},{10,9},{11,10},{13,12},{... | collective-permute-start | bytes 491528 | tf_op jit(solution)/shard_map/ppermute | solution.py:20
  52.1 24.7 %copy-start.6 = (bf16[8,16,16,512]{3,2,1,0:T(8,128)(2,1)}, bf16[8,16,16,512]{3,2,1,0:T(8,128)(2,1)S(1)}, u32[]{:S(2)}) copy-start(bf16[8,16,16,512]{3,2,1,0:T(8,128)(2,1)S(1)} %add_convert_fusion) | copy-start | bytes 6291460
  54.7 92.0 %copy-start.2 = (f32[1024,2048]{1,0:T(8,128)}, f32[1024,2048]{1,0:T(8,128)S(1)}, u32[]{:S(2)}) copy-start(f32[1024,2048]{1,0:T(8,128)S(1)} %get-tuple-element.55) | copy-start | bytes 25165828
  56.1 92.5 %copy-start.3 = (f32[1024,2048]{1,0:T(8,128)}, f32[1024,2048]{1,0:T(8,128)S(1)}, u32[]{:S(2)}) copy-start(f32[1024,2048]{1,0:T(8,128)S(1)} %get-tuple-element.53) | copy-start | bytes 25165828
  72.3 4.5 %copy-start.13 = (bf16[512,512]{1,0:T(8,128)(2,1)S(1)}, bf16[512,512]{1,0:T(8,128)(2,1)}, u32[]{:S(2)}) copy-start(bf16[512,512]{1,0:T(8,128)(2,1)} %param.18) | copy-start | bytes 1572868
  154.3 20.8 %all-to-all-start.1 = ((f32[32,1,256]{2,1,0:T(1,128)}), f32[32,1,256]{2,1,0:T(1,128)S(1)}, u32[]{:S(2)}, u32[]{:S(2)}) async-start(f32[32,1,256]{2,1,0:T(1,128)} %reshape.112), calls=%async_computation.1 | async-start | bytes 65536 | tf_op jit(solution)/shard_map/all_to_all | solution.py:121
  175.1 17.8 %all-to-all-start.2 = ((f32[32,1,256]{2,1,0:T(1,128)}), f32[32,1,256]{2,1,0:T(1,128)S(1)}, u32[]{:S(2)}, u32[]{:S(2)}) async-start(f32[32,1,256]{2,1,0:T(1,128)} %reshape.114), calls=%async_computation.2 | async-start | bytes 65536 | tf_op jit(solution)/shard_map/all_to_all | solution.py:120
  192.9 54.7 %all-to-all-start = ((f32[1,1024,512]{2,0,1:T(1,128)}), f32[1,1024,512]{2,0,1:T(1,128)}, u32[]{:S(2)}, u32[]{:S(2)}) async-start(f32[1,1024,512]{2,0,1:T(1,128)} %copy.23), calls=%async_computation | async-start | bytes 4194304 | tf_op jit(solution)/shard_map/all_to_all | solution.py:119
  198.9 105.8 %all-gather.2.cloned.1.call-start = ((), (), s32[]{:S(2)}) async-start(), calls=%async_computation.3 | async-start | bytes 1081344 | tf_op jit(solution)/shard_map/all_gather | solution.py:136
  209.4 40.4 %copy-start.8 = (bf16[512,512]{1,0:T(8,128)(2,1)S(1)}, bf16[512,512]{1,0:T(8,128)(2,1)}, u32[]{:S(2)}) copy-start(bf16[512,512]{1,0:T(8,128)(2,1)} %param.19) | copy-start | bytes 1572868
  209.5 42.0 %copy-start.14 = (bf16[512,512]{1,0:T(8,128)(2,1)S(1)}, bf16[512,512]{1,0:T(8,128)(2,1)}, u32[]{:S(2)}) copy-start(bf16[512,512]{1,0:T(8,128)(2,1)} %param.20) | copy-start | bytes 1572868
  251.4 53.2 %copy-start.15 = (bf16[512,512]{1,0:T(8,128)(2,1)S(1)}, bf16[512,512]{1,0:T(8,128)(2,1)}, u32[]{:S(2)}) copy-start(bf16[512,512]{1,0:T(8,128)(2,1)} %param.21) | copy-start | bytes 1572868
  357.0 5.1 %copy-start.11 = (bf16[1024,512]{1,0:T(8,128)(2,1)S(1)}, bf16[1024,512]{1,0:T(8,128)(2,1)}, u32[]{:S(2)}) copy-start(bf16[1024,512]{1,0:T(8,128)(2,1)} %all-gather.2.cloned.1.call-done) | copy-start | bytes 3145732
  357.0 5.1 %copy-start.16 = (bf16[512,512]{1,0:T(8,128)(2,1)S(1)}, bf16[512,512]{1,0:T(8,128)(2,1)}, u32[]{:S(2)}) copy-start(bf16[512,512]{1,0:T(8,128)(2,1)} %param.22) | copy-start | bytes 1572868
  372.7 10.2 %slice-start = ((s8[8388608]{0:T(1024)(128)(4,1)}), s8[4194304]{0:T(1024)(128)(4,1)S(1)}, s32[]{:S(2)}) async-start(s8[8388608]{0:T(1024)(128)(4,1)} %bitcast.74), calls=%async_computation.4 | async-start | bytes 8388608
  377.8 5.1 %slice-start.1 = ((s8[8388608]{0:T(1024)(128)(4,1)}), s8[4194304]{0:T(1024)(128)(4,1)S(1)}, s32[]{:S(2)}) async-start(s8[8388608]{0:T(1024)(128)(4,1)} %bitcast.74), calls=%async_computation.5 | async-start | bytes 8388608
  387.6 1.6 copy-start.5
  387.6 1.7 copy-start.7
  387.6 5.0 %copy-start.1 = (bf16[512,512]{1,0:T(8,128)(2,1)S(1)}, bf16[512,512]{1,0:T(8,128)(2,1)}, u32[]{:S(2)}) copy-start(bf16[512,512]{1,0:T(8,128)(2,1)} %param.17) | copy-start | bytes 1572868
Sparse Core Ops, SparseCore 0:
  251.5 53.0 all-gather.1
where the time goes:
time: 405 us; the launch traced here: 400 us
  matrix products  154 us (38%)
  waiting for transfers between devices  101 us (25%)
  other arithmetic  82.8 us (20%)
  starting transfers between devices  30.2 us (7%)
  local copies, waits for them, and re-layouts  17.8 us (4%)
  between operations  14.2 us (4%)
    dot_general x8, matrix products, exact_dot(): jnp.dot(weights, values_block, precision=lax.Precision.HIGHEST, preferred...  61.6 us
    dot_general x16, matrix products, pair_scores(): lax.dot_general(queries, key_rows, (((1,), (1,)), ((), ())), preferred_el...  50.3 us
    all_gather x1, waiting for transfers between devices, per_device(): lax.all_gather(own_state, ('wide', 'narrow'), axis=0, tiled=True)  50.3 us
    all_to_all x1, waiting for transfers between devices, per_device(): lax.all_to_all(summed1, ('wide', 'narrow'), split_axis=1, concat_axis=0,...  38.1 us
    reduce_sum x8, other arithmetic, per_device(): totals = jnp.sum(weights, axis=1, keepdims=True)  28.4 us
    dot_general x8, matrix products, per_device(): jnp.dot(weights.astype(jnp.bfloat16), head_block(values2, head_index, hea...  26.2 us
    reduce_sum x8, other arithmetic, per_device(): totals_list.append(jnp.sum(weights, axis=1))  25.6 us
    convert_element_type x1, other arithmetic, per_device(): mixed_cells = stencil.astype(jnp.bfloat16).reshape(cell_count, model_width)  16.4 us
  transfers between devices with their start and end apart: 8, of which 4 were waited for; matrix products, arithmetic and copies ran while one was open for 9% of the time, Pallas kernels for 0%

commit v1 on v0

--- a/solution.py
+++ b/solution.py
@@ -5,6 +5,18 @@
 from jax.sharding import PartitionSpec as P
 
 HEADS = 8
+
+
+def gather_by_bits(array, axis, dim):
+    ways, here = (lax.axis_size(axis), lax.axis_index(axis))
+    grown, reach = (array, 1)
+    while reach < ways:
+        theirs = lax.ppermute(grown, axis, [(d, d ^ reach) for d in range(ways)])
+        mine_first = jnp.concatenate([grown, theirs], axis=dim)
+        theirs_first = jnp.concatenate([theirs, grown], axis=dim)
+        grown = jnp.where(here & reach == 0, mine_first, theirs_first)
+        reach = 2 * reach
+    return grown
 
 
 def padded_2(cells, sides, width):
@@ -133,7 +145,7 @@
     ) * row_count
     own_latents = lax.dynamic_slice_in_dim(latents, start, row_count, 0)
     own_state = update_state(summed, totals, own_latents, w_out1, head_count)
-    latent_state = lax.all_gather(own_state, ("wide", "narrow"), axis=0, tiled=True)
+    latent_state = gather_by_bits(own_state, ("wide", "narrow"), 0)
     keys2 = project(latent_state, w_key2)
     values2 = project(latent_state, w_value2)
     queries2 = project(mixed_cells, w_query2)

time: 405 us -> 376 us (0.928)
  waiting for transfers between devices: 101 us -> 83.2 us
  between operations: 14.2 us -> 0.79 us
  starting transfers between devices: 30.2 us -> 34.6 us
    all_gather x1 -> x0, waiting for transfers between devices: 50.3 us -> none  [per_device(): lax.all_gather(own_state, ('wide', 'narrow'), axis=0, tiled=True)]
    ppermute x0 -> x5, waiting for transfers between devices: none -> 32.4 us  [gather_by_bits(): theirs = lax.ppermute(grown, axis, [(d, d ^ reach) for d in range(ways)])]
    ppermute x0 -> x5, starting transfers between devices: none -> 4.43 us  [gather_by_bits(): theirs = lax.ppermute(grown, axis, [(d, d ^ reach) for d in range(ways)])]
  transfers between devices with their start and end apart: 8 -> 12, of which waited for: 4 -> 8; matrix products, arithmetic and copies ran while one was open for 9% -> 10% of each run, Pallas kernels for 0% -> 0%
where the time goes in v1:
time: 376 us; the launch traced here: 371 us
  matrix products  152 us (40%)
  waiting for transfers between devices  83.2 us (22%)
  other arithmetic  83.1 us (22%)
  starting transfers between devices  34.6 us (9%)
  local copies, waits for them, and re-layouts  17.8 us (5%)
    dot_general x8, matrix products, exact_dot(): jnp.dot(weights, values_block, precision=lax.Precision.HIGHEST, preferred...  61.6 us
    dot_general x16, matrix products, pair_scores(): lax.dot_general(queries, key_rows, (((1,), (1,)), ((), ())), preferred_el...  50.3 us
    all_to_all x1, waiting for transfers between devices, per_device(): lax.all_to_all(summed1, ('wide', 'narrow'), split_axis=1, concat_axis=0,...  38.1 us
    ppermute x5, waiting for transfers between devices, gather_by_bits(): theirs = lax.ppermute(grown, axis, [(d, d ^ reach) for d in range(ways)])  32.4 us
    reduce_sum x8, other arithmetic, per_device(): totals = jnp.sum(weights, axis=1, keepdims=True)  28.4 us
    dot_general x8, matrix products, per_device(): jnp.dot(weights.astype(jnp.bfloat16), head_block(values2, head_index, hea...  26.2 us
    reduce_sum x8, other arithmetic, per_device(): totals_list.append(jnp.sum(weights, axis=1))  25.6 us
    convert_element_type x1, other arithmetic, per_device(): mixed_cells = stencil.astype(jnp.bfloat16).reshape(cell_count, model_width)  16.4 us
  transfers between devices with their start and end apart: 12, of which 8 were waited for; matrix products, arithmetic and copies ran while one was open for 10% of the time, Pallas kernels for 0%

profile of v1, /device:TPU:0, one launch (start us, length us, event | category | flops | bytes accessed | tf_op | source)
XLA Modules:
  0.0 371.2 jit_solution(16370202451617796810)
XLA Ops:
  1.0 1.9 broadcast_multiply_fusion
  3.0 4.9 %collective-permute-start = (bf16[1,16,16,512]{3,2,1,0:T(8,128)(2,1)S(1)}, bf16[1,16,16,512]{3,2,1,0:T(8,128)(2,1)S(1)}, u32[]{:S(2)}, u32[]{:S(2)}) collective-permute-start(bf16[1,16,16,512]{3,2,1,0:T(8,128)(2,1)S(1)} %get-tuple-element.11), channel_id=1, source_target_pairs={{0,4},{4,8},{8,12},{12,16},{16,20},{20,24},{24,28},{1,5},{5,9},{9,... | collective-permute-start | bytes 786440 | tf_op jit(solution)/shard_map/ppermute | solution.py:30
  10.0 9.0 %collective-permute-done = bf16[1,16,16,512]{3,2,1,0:T(8,128)(2,1)S(1)} collective-permute-done((bf16[1,16,16,512]{3,2,1,0:T(8,128)(2,1)S(1)}, bf16[1,16,16,512]{3,2,1,0:T(8,128)(2,1)S(1)}, u32[]{:S(2)}, u32[]{:S(2)}) %collective-permute-start) | collective-permute-done | bytes 262176 | tf_op jit(solution)/shard_map/ppermute | solution.py:30
  21.7 3.7 collective-permute-done.3
  25.4 2.8 select_maximum_fusion
  29.2 16.4 %add_convert_fusion = bf16[8,16,16,512]{3,2,1,0:T(8,128)(2,1)S(1)} fusion(bf16[8,16,16,512]{3,2,1,0:T(8,128)(2,1)S(1)} %broadcast_multiply_fusion, bf16[10,18,18,512]{3,2,1,0:T(8,128)(2,1)S(1)} %select_maximum_fusion, bf16[10,17,16,512]{3,2,1,0:T(8,128)(2,1)S(1)} %get-tuple-element.8, bf16[1,16,16,512]{3,2,1,0:T(8,128)(2,1)S(1)} %collective-permute-done.1, ...), kind=kLoop, calls=%fused_computation.91 | loop fusion | flops 88080384 | bytes 55105536 | tf_op jit(solution)/shard_map/convert_element_type | solution.py:106
  52.3 4.5 %multiply_reduce_fusion.12 = (f32[1024]{0:T(1024)S(1)}, f32[1024,2048]{1,0:T(8,128)}) fusion(bf16[2048,512]{0,1:T(8,128)(2,1)S(1)} %convolution_convert_fusion.1, bf16[1024,512]{0,1:T(8,128)(2,1)S(1)} %convolution_convert_fusion.5), kind=kOutput, calls=%fused_computation.31 | convolution fusion | flops 272628736 | bytes 8785920 | tf_op jit(solution)/shard_map/dot_general | solution.py:45
  56.8 4.5 %multiply_reduce_fusion.13 = (f32[1024]{0:T(1024)S(1)}, f32[1024,2048]{1,0:T(8,128)}) fusion(bf16[2048,512]{0,1:T(8,128)(2,1)S(1)} %convolution_convert_fusion.1, bf16[1024,512]{0,1:T(8,128)(2,1)S(1)} %convolution_convert_fusion.5), kind=kOutput, calls=%fused_computation.32 | convolution fusion | flops 272628736 | bytes 8785920 | tf_op jit(solution)/shard_map/dot_general | solution.py:45
  61.3 4.5 %multiply_reduce_fusion.14 = (f32[1024]{0:T(1024)S(1)}, f32[1024,2048]{1,0:T(8,128)}) fusion(bf16[2048,512]{0,1:T(8,128)(2,1)S(1)} %convolution_convert_fusion.1, bf16[1024,512]{0,1:T(8,128)(2,1)S(1)} %convolution_convert_fusion.5), kind=kOutput, calls=%fused_computation.33 | convolution fusion | flops 272628736 | bytes 8785920 | tf_op jit(solution)/shard_map/dot_general | solution.py:45
  65.8 4.5 %multiply_reduce_fusion.15 = (f32[1024]{0:T(1024)S(1)}, f32[1024,2048]{1,0:T(8,128)}) fusion(bf16[2048,512]{0,1:T(8,128)(2,1)S(1)} %convolution_convert_fusion.1, bf16[1024,512]{0,1:T(8,128)(2,1)S(1)} %convolution_convert_fusion.5), kind=kOutput, calls=%fused_computation.34 | convolution fusion | flops 272628736 | bytes 8785920 | tf_op jit(solution)/shard_map/dot_general | solution.py:45
  70.3 2.8 convolution_convert_fusion
  73.1 4.4 %fusion.1 = f32[1024]{0:T(1024)S(1)} fusion(f32[1024,2048]{1,0:T(8,128)} %get-tuple-element.41, f32[1024]{0:T(1024)S(1)} %get-tuple-element.40), kind=kLoop, calls=%fused_computation.35 | loop fusion | flops 6290432 | bytes 8396800 | tf_op jit(solution)/shard_map/reduce_sum | solution.py:125
  77.4 7.9 %fusion.149 = f32[1024,512]{0,1:T(8,128)S(1)} fusion(f32[1024,2048]{1,0:T(8,128)} %get-tuple-element.41, f32[1024]{0:T(1024)S(1)} %get-tuple-element.40, bf16[2048,512]{0,1:T(8,128)(2,1)} %convolution_convert_fusion), kind=kOutput, calls=%fused_computation.142 | convolution fusion | flops 1614807040 | bytes 8916992 | tf_op jit(solution)/shard_map/dot_general | solution.py:55
  85.3 4.4 %fusion.3 = f32[1024]{0:T(1024)S(1)} fusion(f32[1024,2048]{1,0:T(8,128)} %get-tuple-element.43, f32[1024]{0:T(1024)S(1)} %get-tuple-element.42), kind=kLoop, calls=%fused_computation.37 | loop fusion | flops 6290432 | bytes 8396800 | tf_op jit(solution)/shard_map/reduce_sum | solution.py:125
  89.7 8.1 %fusion.148 = f32[1024,512]{0,1:T(8,128)S(1)} fusion(f32[1024,512]{0,1:T(8,128)S(1)} %fusion.149, f32[1024,2048]{1,0:T(8,128)} %get-tuple-element.43, f32[1024]{0:T(1024)S(1)} %get-tuple-element.42, bf16[2048,512]{0,1:T(8,128)(2,1)} %convolution_convert_fusion), kind=kOutput, calls=%fused_computation.141 | convolution fusion | flops 1614807040 | bytes 8916992 | tf_op jit(solution)/shard_map/dot_general | solution.py:55
  97.8 4.4 %fusion.5 = f32[1024]{0:T(1024)S(1)} fusion(f32[1024,2048]{1,0:T(8,128)} %get-tuple-element.45, f32[1024]{0:T(1024)S(1)} %get-tuple-element.44), kind=kLoop, calls=%fused_computation.39 | loop fusion | flops 6290432 | bytes 8396800 | tf_op jit(solution)/shard_map/reduce_sum | solution.py:125
  102.1 8.1 %fusion.147 = f32[1024,512]{0,1:T(8,128)S(1)} fusion(f32[1024,512]{0,1:T(8,128)S(1)} %fusion.148, f32[1024,2048]{1,0:T(8,128)} %get-tuple-element.45, f32[1024]{0:T(1024)S(1)} %get-tuple-element.44, bf16[2048,512]{0,1:T(8,128)(2,1)} %convolution_convert_fusion), kind=kOutput, calls=%fused_computation.140 | convolution fusion | flops 1614807040 | bytes 8916992 | tf_op jit(solution)/shard_map/dot_general | solution.py:55
  110.3 4.4 %fusion.7 = f32[1024]{0:T(1024)S(1)} fusion(f32[1024,2048]{1,0:T(8,128)} %get-tuple-element.47, f32[1024]{0:T(1024)S(1)} %get-tuple-element.46), kind=kLoop, calls=%fused_computation.41 | loop fusion | flops 6290432 | bytes 8396800 | tf_op jit(solution)/shard_map/reduce_sum | solution.py:125
  114.6 8.3 %fusion.146 = f32[1024,512]{0,1:T(8,128)S(1)} fusion(f32[1024,512]{0,1:T(8,128)S(1)} %fusion.147, f32[1024,2048]{1,0:T(8,128)} %get-tuple-element.47, f32[1024]{0:T(1024)S(1)} %get-tuple-element.46, bf16[2048,512]{0,1:T(8,128)(2,1)} %convolution_convert_fusion), kind=kOutput, calls=%fused_computation.139 | convolution fusion | flops 1614807040 | bytes 8916992 | tf_op jit(solution)/shard_map/dot_general | solution.py:55
  123.0 1.9 fusion.9
  124.9 6.5 %fusion.145 = f32[1024,512]{0,1:T(8,128)S(1)} fusion(f32[1024,512]{0,1:T(8,128)S(1)} %fusion.146, f32[1024,2048]{1,0:T(8,128)S(1)} %get-tuple-element.49, f32[1024]{0:T(1024)S(1)} %get-tuple-element.48, bf16[2048,512]{0,1:T(8,128)(2,1)} %convolution_convert_fusion), kind=kOutput, calls=%fused_computation.138 | convolution fusion | flops 1614807040 | bytes 8916992 | tf_op jit(solution)/shard_map/dot_general | solution.py:55
  131.4 2.3 fusion.11
  133.7 6.5 %fusion.144 = f32[1024,512]{0,1:T(8,128)S(1)} fusion(f32[1024,512]{0,1:T(8,128)S(1)} %fusion.145, f32[1024,2048]{1,0:T(8,128)S(1)} %get-tuple-element.51, f32[1024]{0:T(1024)S(1)} %get-tuple-element.50, bf16[2048,512]{0,1:T(8,128)(2,1)} %convolution_convert_fusion), kind=kOutput, calls=%fused_computation.137 | convolution fusion | flops 1614807040 | bytes 8916992 | tf_op jit(solution)/shard_map/dot_general | solution.py:55
  140.2 1.9 fusion.15
  142.1 1.9 fusion.13
  145.0 1.9 reduce.3
  147.8 9.5 %all-to-all-start.1 = ((f32[32,1,256]{2,1,0:T(1,128)}), f32[32,1,256]{2,1,0:T(1,128)S(1)}, u32[]{:S(2)}, u32[]{:S(2)}) async-start(f32[32,1,256]{2,1,0:T(1,128)} %reshape.112), calls=%async_computation.1 | async-start | bytes 65536 | tf_op jit(solution)/shard_map/all_to_all | solution.py:133
  157.3 8.1 %fusion.143 = f32[1024,512]{0,1:T(8,128)S(1)} fusion(f32[1024,512]{0,1:T(8,128)S(1)} %fusion.144, f32[1024,2048]{1,0:T(8,128)} %copy-done.3, f32[1024]{0:T(1024)S(1)} %get-tuple-element.52, bf16[2048,512]{0,1:T(8,128)(2,1)} %convolution_convert_fusion), kind=kOutput, calls=%fused_computation.136 | convolution fusion | flops 1614807040 | bytes 8916992 | tf_op jit(solution)/shard_map/dot_general | solution.py:55
  165.8 1.9 reduce.1
  168.6 5.9 %all-to-all-start.2 = ((f32[32,1,256]{2,1,0:T(1,128)}), f32[32,1,256]{2,1,0:T(1,128)S(1)}, u32[]{:S(2)}, u32[]{:S(2)}) async-start(f32[32,1,256]{2,1,0:T(1,128)} %reshape.114), calls=%async_computation.2 | async-start | bytes 65536 | tf_op jit(solution)/shard_map/all_to_all | solution.py:132
  174.6 8.1 %fusion.142 = f32[1024,512]{0,1:T(8,128)S(1)} fusion(f32[1024,512]{0,1:T(8,128)S(1)} %fusion.143, f32[1024,2048]{1,0:T(8,128)} %copy-done.2, f32[1024]{0:T(1024)S(1)} %get-tuple-element.54, bf16[2048,512]{0,1:T(8,128)(2,1)} %convolution_convert_fusion), kind=kOutput, calls=%fused_computation.135 | convolution fusion | flops 1614807040 | bytes 8916992 | tf_op jit(solution)/shard_map/dot_general | solution.py:55
  182.7 3.7 copy.23
  186.4 6.0 %all-to-all-start = ((f32[1,1024,512]{2,0,1:T(1,128)}), f32[1,1024,512]{2,0,1:T(1,128)}, u32[]{:S(2)}, u32[]{:S(2)}) async-start(f32[1,1024,512]{2,0,1:T(1,128)} %copy.23), calls=%async_computation | async-start | bytes 4194304 | tf_op jit(solution)/shard_map/all_to_all | solution.py:131
  196.6 2.6 mul.452
  199.2 3.6 mul.453
  202.9 38.1 %all-to-all-done = f32[1,1024,512]{2,0,1:T(1,128)} async-done(((f32[1,1024,512]{2,0,1:T(1,128)}), f32[1,1024,512]{2,0,1:T(1,128)}, u32[]{:S(2)}, u32[]{:S(2)}) %all-to-all-start) | async-done | bytes 2097184 | tf_op jit(solution)/shard_map/all_to_all | solution.py:131
  241.0 1.8 copy.31
  245.5 1.5 collective-permute-start.5
  247.0 2.8 collective-permute-done.5
  249.9 1.5 collective-permute-start.6
  251.4 3.5 collective-permute-done.6
  255.2 6.2 %collective-permute-done.7 = bf16[256,512]{1,0:T(8,128)(2,1)S(1)} collective-permute-done((bf16[256,512]{1,0:T(8,128)(2,1)S(1)}, bf16[256,512]{1,0:T(8,128)(2,1)S(1)}, u32[]{:S(2)}, u32[]{:S(2)}) %collective-permute-start.7) | collective-permute-done | bytes 262176 | tf_op jit(solution)/shard_map/ppermute | solution.py:14
  262.8 2.9 convolution_convert_fusion.2
  265.8 18.6 %collective-permute-done.8 = bf16[512,512]{1,0:T(8,128)(2,1)S(1)} collective-permute-done((bf16[512,512]{1,0:T(8,128)(2,1)S(1)}, bf16[512,512]{1,0:T(8,128)(2,1)S(1)}, u32[]{:S(2)}, u32[]{:S(2)}) %collective-permute-start.8) | collective-permute-done | bytes 524320 | tf_op jit(solution)/shard_map/ppermute | solution.py:14
  289.1 4.5 %multiply_reduce_fusion.3 = (f32[2048]{0:T(1024)S(1)}, f32[2048,1024]{0,1:T(8,128)}) fusion(bf16[1024,512]{0,1:T(8,128)(2,1)S(1)} %convolution_convert_fusion.4, bf16[2048,512]{0,1:T(8,128)(2,1)S(1)} %convolution_convert_fusion.2), kind=kOutput, calls=%fused_computation.22 | convolution fusion | flops 272627712 | bytes 8790016 | tf_op jit(solution)/shard_map/dot_general | solution.py:45
  293.6 4.5 %multiply_reduce_fusion.4 = (f32[2048]{0:T(1024)S(1)}, f32[2048,1024]{0,1:T(8,128)}) fusion(bf16[1024,512]{0,1:T(8,128)(2,1)S(1)} %convolution_convert_fusion.4, bf16[2048,512]{0,1:T(8,128)(2,1)S(1)} %convolution_convert_fusion.2), kind=kOutput, calls=%fused_computation.23 | convolution fusion | flops 272627712 | bytes 8790016 | tf_op jit(solution)/shard_map/dot_general | solution.py:45
  298.1 4.5 %multiply_reduce_fusion.5 = (f32[2048]{0:T(1024)S(1)}, f32[2048,1024]{0,1:T(8,128)}) fusion(bf16[1024,512]{0,1:T(8,128)(2,1)S(1)} %convolution_convert_fusion.4, bf16[2048,512]{0,1:T(8,128)(2,1)S(1)} %convolution_convert_fusion.2), kind=kOutput, calls=%fused_computation.24 | convolution fusion | flops 272627712 | bytes 8790016 | tf_op jit(solution)/shard_map/dot_general | solution.py:45
  302.6 5.0 %multiply_reduce_fusion.6 = (f32[2048]{0:T(1024)S(1)}, f32[2048,1024]{0,1:T(8,128)}) fusion(bf16[1024,512]{0,1:T(8,128)(2,1)S(1)} %convolution_convert_fusion.4, bf16[2048,512]{0,1:T(8,128)(2,1)S(1)} %convolution_convert_fusion.2), kind=kOutput, calls=%fused_computation.25 | convolution fusion | flops 272627712 | bytes 8790016 | tf_op jit(solution)/shard_map/dot_general | solution.py:45
  307.6 4.5 %multiply_reduce_fusion.7 = (f32[2048]{0:T(1024)S(1)}, f32[2048,1024]{0,1:T(8,128)}) fusion(bf16[1024,512]{0,1:T(8,128)(2,1)S(1)} %convolution_convert_fusion.4, bf16[2048,512]{0,1:T(8,128)(2,1)S(1)} %convolution_convert_fusion.2), kind=kOutput, calls=%fused_computation.26 | convolution fusion | flops 272627712 | bytes 8790016 | tf_op jit(solution)/shard_map/dot_general | solution.py:45
  313.5 1.4 fusion.29
  316.3 4.8 %fusion.25 = f32[2048]{0:T(1024)S(1)} fusion(f32[2048,1024]{0,1:T(8,128)} %get-tuple-element.65, f32[2048]{0:T(1024)S(1)} %get-tuple-element.64), kind=kLoop, calls=%fused_computation.59 | loop fusion | flops 6289408 | bytes 8404992 | tf_op jit(solution)/shard_map/reduce_sum | solution.py:161
  321.1 4.8 %fusion.23 = f32[2048]{0:T(1024)S(1)} fusion(f32[2048,1024]{0,1:T(8,128)} %get-tuple-element.63, f32[2048]{0:T(1024)S(1)} %get-tuple-element.62), kind=kLoop, calls=%fused_computation.57 | loop fusion | flops 6289408 | bytes 8404992 | tf_op jit(solution)/shard_map/reduce_sum | solution.py:161
  325.9 4.8 %fusion.21 = f32[2048]{0:T(1024)S(1)} fusion(f32[2048,1024]{0,1:T(8,128)} %get-tuple-element.61, f32[2048]{0:T(1024)S(1)} %get-tuple-element.60), kind=kLoop, calls=%fused_computation.55 | loop fusion | flops 6289408 | bytes 8404992 | tf_op jit(solution)/shard_map/reduce_sum | solution.py:161
  330.7 4.8 %fusion.19 = f32[2048]{0:T(1024)S(1)} fusion(f32[2048,1024]{0,1:T(8,128)} %get-tuple-element.59, f32[2048]{0:T(1024)S(1)} %get-tuple-element.58), kind=kLoop, calls=%fused_computation.53 | loop fusion | flops 6289408 | bytes 8404992 | tf_op jit(solution)/shard_map/reduce_sum | solution.py:161
  335.5 5.0 %fusion.17 = f32[2048]{0:T(1024)S(1)} fusion(f32[2048,1024]{0,1:T(8,128)} %get-tuple-element.57, f32[2048]{0:T(1024)S(1)} %get-tuple-element.56), kind=kLoop, calls=%fused_computation.51 | loop fusion | flops 6289408 | bytes 8404992 | tf_op jit(solution)/shard_map/reduce_sum | solution.py:161
  341.3 4.9 %fusion.76 = bf16[2048,512]{0,1:T(8,128)(2,1)S(1)} fusion(f32[2048,1024]{0,1:T(8,128)} %get-tuple-element.57, f32[2048]{0:T(1024)S(1)} %get-tuple-element.56, f32[2048]{0:T(1024)S(1)} %fusion.17, bf16[1024,512]{0,1:T(8,128)(2,1)S(1)} %convolution_convert_fusion.3), kind=kOutput, calls=%fused_computation.107 | convolution fusion | flops 274989056 | bytes 8798208 | tf_op jit(solution)/shard_map/dot_general | solution.py:162
  346.2 4.9 %fusion.85 = bf16[2048,512]{0,1:T(8,128)(2,1)S(1)} fusion(bf16[2048,512]{0,1:T(8,128)(2,1)S(1)} %fusion.76, f32[2048,1024]{0,1:T(8,128)} %get-tuple-element.59, f32[2048]{0:T(1024)S(1)} %get-tuple-element.58, f32[2048]{0:T(1024)S(1)} %fusion.19, bf16[1024,512]{0,1:T(8,128)(2,1)S(1)} %convolution_convert_fusion.3), kind=kOutput, calls=%fused_computation.110 | convolution fusion | flops 274989056 | bytes 8798208 | tf_op jit(solution)/shard_map/dot_general | solution.py:162
  351.1 5.1 %fusion.94 = bf16[2048,512]{0,1:T(8,128)(2,1)S(1)} fusion(bf16[2048,512]{0,1:T(8,128)(2,1)S(1)} %fusion.85, f32[2048,1024]{0,1:T(8,128)} %get-tuple-element.61, f32[2048]{0:T(1024)S(1)} %get-tuple-element.60, f32[2048]{0:T(1024)S(1)} %fusion.21, bf16[1024,512]{0,1:T(8,128)(2,1)S(1)} %convolution_convert_fusion.3), kind=kOutput, calls=%fused_computation.113 | convolution fusion | flops 274989056 | bytes 8798208 | tf_op jit(solution)/shard_map/dot_general | solution.py:162
  356.2 5.1 %fusion.103 = bf16[2048,512]{0,1:T(8,128)(2,1)S(1)} fusion(bf16[2048,512]{0,1:T(8,128)(2,1)S(1)} %fusion.94, f32[2048,1024]{0,1:T(8,128)} %get-tuple-element.63, f32[2048]{0:T(1024)S(1)} %get-tuple-element.62, f32[2048]{0:T(1024)S(1)} %fusion.23, bf16[1024,512]{0,1:T(8,128)(2,1)S(1)} %convolution_convert_fusion.3), kind=kOutput, calls=%fused_computation.116 | convolution fusion | flops 274989056 | bytes 8798208 | tf_op jit(solution)/shard_map/dot_general | solution.py:162
  361.3 1.6 fusion.112
  362.9 1.6 fusion.121
  364.4 1.6 fusion.130
  366.0 1.5 fusion.139
  367.7 3.3 bitcast_add_fusion
  (93 shorter events, 33.5 us)
Async XLA Ops:
  0.0 45.6 %copy-start = (bf16[512,512]{1,0:T(8,128)(2,1)S(1)}, bf16[512,512]{1,0:T(8,128)(2,1)}, u32[]{:S(2)}) copy-start(bf16[512,512]{1,0:T(8,128)(2,1)} %param.17) | copy-start | bytes 1572868
  0.0 9.2 %copy-start.9 = (f32[27,512]{1,0:T(8,128)S(1)}, f32[27,512]{1,0:T(8,128)}, u32[]{:S(2)}) copy-start(f32[27,512]{1,0:T(8,128)} %param.14) | copy-start | bytes 165892
  0.0 9.3 %copy-start.10 = (bf16[1024,512]{1,0:T(8,128)(2,1)S(1)}, bf16[1024,512]{1,0:T(8,128)(2,1)}, u32[]{:S(2)}) copy-start(bf16[1024,512]{1,0:T(8,128)(2,1)} %param.15) | copy-start | bytes 3145732
  0.0 9.3 %copy-start.11 = (bf16[512,512]{1,0:T(8,128)(2,1)S(1)}, bf16[512,512]{1,0:T(8,128)(2,1)}, u32[]{:S(2)}) copy-start(bf16[512,512]{1,0:T(8,128)(2,1)} %param.16) | copy-start | bytes 1572868
  2.9 26.2 %copy-start.4 = (bf16[8,16,16,512]{3,2,1,0:T(8,128)(2,1)}, bf16[8,16,16,512]{3,2,1,0:T(8,128)(2,1)S(1)}, u32[]{:S(2)}) copy-start(bf16[8,16,16,512]{3,2,1,0:T(8,128)(2,1)S(1)} %broadcast_multiply_fusion) | copy-start | bytes 6291460
  3.0 16.1 %collective-permute-start = (bf16[1,16,16,512]{3,2,1,0:T(8,128)(2,1)S(1)}, bf16[1,16,16,512]{3,2,1,0:T(8,128)(2,1)S(1)}, u32[]{:S(2)}, u32[]{:S(2)}) collective-permute-start(bf16[1,16,16,512]{3,2,1,0:T(8,128)(2,1)S(1)} %get-tuple-element.11), channel_id=1, source_target_pairs={{0,4},{4,8},{8,12},{12,16},{16,20},{20,24},{24,28},{1,5},{5,9},{9,... | collective-permute-start | bytes 786440 | tf_op jit(solution)/shard_map/ppermute | solution.py:30
  7.9 11.2 %collective-permute-start.1 = (bf16[1,16,16,512]{3,2,1,0:T(8,128)(2,1)S(1)}, bf16[1,16,16,512]{3,2,1,0:T(8,128)(2,1)S(1)}, u32[]{:S(2)}, u32[]{:S(2)}) collective-permute-start(bf16[1,16,16,512]{3,2,1,0:T(8,128)(2,1)S(1)} %get-tuple-element.12), channel_id=1, source_target_pairs={{4,0},{8,4},{12,8},{16,12},{20,16},{24,20},{28,24},{5,1},{9,5},{13... | collective-permute-start | bytes 786440 | tf_op jit(solution)/shard_map/ppermute | solution.py:32
  19.1 2.6 collective-permute-start.2
  20.4 5.0 %collective-permute-start.3 = (bf16[10,1,16,512]{3,2,1,0:T(8,128)(2,1)S(1)}, bf16[10,1,16,512]{3,2,1,0:T(8,128)(2,1)S(1)}, u32[]{:S(2)}, u32[]{:S(2)}) collective-permute-start(bf16[10,1,16,512]{3,2,1,0:T(8,128)(2,1)S(1)} %get-tuple-element.10), channel_id=1, source_target_pairs={{1,0},{2,1},{3,2},{5,4},{6,5},{7,6},{9,8},{10,9},{11,10},{13,12},{... | collective-permute-start | bytes 491528 | tf_op jit(solution)/shard_map/ppermute | solution.py:32
  45.5 24.7 %copy-start.6 = (bf16[8,16,16,512]{3,2,1,0:T(8,128)(2,1)}, bf16[8,16,16,512]{3,2,1,0:T(8,128)(2,1)S(1)}, u32[]{:S(2)}) copy-start(bf16[8,16,16,512]{3,2,1,0:T(8,128)(2,1)S(1)} %add_convert_fusion) | copy-start | bytes 6291460
  48.2 92.0 %copy-start.2 = (f32[1024,2048]{1,0:T(8,128)}, f32[1024,2048]{1,0:T(8,128)S(1)}, u32[]{:S(2)}) copy-start(f32[1024,2048]{1,0:T(8,128)S(1)} %get-tuple-element.55) | copy-start | bytes 25165828
  49.6 92.5 %copy-start.3 = (f32[1024,2048]{1,0:T(8,128)}, f32[1024,2048]{1,0:T(8,128)S(1)}, u32[]{:S(2)}) copy-start(f32[1024,2048]{1,0:T(8,128)S(1)} %get-tuple-element.53) | copy-start | bytes 25165828
  65.8 4.5 %copy-start.12 = (bf16[512,512]{1,0:T(8,128)(2,1)S(1)}, bf16[512,512]{1,0:T(8,128)(2,1)}, u32[]{:S(2)}) copy-start(bf16[512,512]{1,0:T(8,128)(2,1)} %param.18) | copy-start | bytes 1572868
  147.8 20.8 %all-to-all-start.1 = ((f32[32,1,256]{2,1,0:T(1,128)}), f32[32,1,256]{2,1,0:T(1,128)S(1)}, u32[]{:S(2)}, u32[]{:S(2)}) async-start(f32[32,1,256]{2,1,0:T(1,128)} %reshape.112), calls=%async_computation.1 | async-start | bytes 65536 | tf_op jit(solution)/shard_map/all_to_all | solution.py:133
  168.6 17.8 %all-to-all-start.2 = ((f32[32,1,256]{2,1,0:T(1,128)}), f32[32,1,256]{2,1,0:T(1,128)S(1)}, u32[]{:S(2)}, u32[]{:S(2)}) async-start(f32[32,1,256]{2,1,0:T(1,128)} %reshape.114), calls=%async_computation.2 | async-start | bytes 65536 | tf_op jit(solution)/shard_map/all_to_all | solution.py:132
  186.4 54.7 %all-to-all-start = ((f32[1,1024,512]{2,0,1:T(1,128)}), f32[1,1024,512]{2,0,1:T(1,128)}, u32[]{:S(2)}, u32[]{:S(2)}) async-start(f32[1,1024,512]{2,0,1:T(1,128)} %copy.23), calls=%async_computation | async-start | bytes 4194304 | tf_op jit(solution)/shard_map/all_to_all | solution.py:131
  202.9 40.4 %copy-start.8 = (bf16[512,512]{1,0:T(8,128)(2,1)S(1)}, bf16[512,512]{1,0:T(8,128)(2,1)}, u32[]{:S(2)}) copy-start(bf16[512,512]{1,0:T(8,128)(2,1)} %param.19) | copy-start | bytes 1572868
  242.8 20.0 %copy-start.13 = (bf16[512,512]{1,0:T(8,128)(2,1)S(1)}, bf16[512,512]{1,0:T(8,128)(2,1)}, u32[]{:S(2)}) copy-start(bf16[512,512]{1,0:T(8,128)(2,1)} %param.20) | copy-start | bytes 1572868
  244.3 1.2 collective-permute-start.4
  245.5 4.3 %collective-permute-start.5 = (bf16[64,512]{1,0:T(8,128)(2,1)S(1)}, bf16[64,512]{1,0:T(8,128)(2,1)S(1)}, u32[]{:S(2)}, u32[]{:S(2)}) collective-permute-start(bf16[64,512]{1,0:T(8,128)(2,1)S(1)} %maximum_select_fusion.6), channel_id=1, source_target_pairs={{0,2},{1,3},{2,0},{3,1},{4,6},{5,7},{6,4},{7,5},{8,10},{9,11},{10,... | collective-permute-start | bytes 196616 | tf_op jit(solution)/shard_map/ppermute | solution.py:14
  249.9 5.0 %collective-permute-start.6 = (bf16[128,512]{1,0:T(8,128)(2,1)S(1)}, bf16[128,512]{1,0:T(8,128)(2,1)S(1)}, u32[]{:S(2)}, u32[]{:S(2)}) collective-permute-start(bf16[128,512]{1,0:T(8,128)(2,1)S(1)} %maximum_select_fusion.5), channel_id=1, source_target_pairs={{0,4},{1,5},{2,6},{3,7},{4,0},{5,1},{6,2},{7,3},{8,12},{9,13},{10,... | collective-permute-start | bytes 393224 | tf_op jit(solution)/shard_map/ppermute | solution.py:14
  255.0 6.4 %collective-permute-start.7 = (bf16[256,512]{1,0:T(8,128)(2,1)S(1)}, bf16[256,512]{1,0:T(8,128)(2,1)S(1)}, u32[]{:S(2)}, u32[]{:S(2)}) collective-permute-start(bf16[256,512]{1,0:T(8,128)(2,1)S(1)} %maximum_select_fusion.2), channel_id=1, source_target_pairs={{0,8},{1,9},{2,10},{3,11},{4,12},{5,13},{6,14},{7,15},{8,0},{9,1},... | collective-permute-start | bytes 786440 | tf_op jit(solution)/shard_map/ppermute | solution.py:14
  261.6 22.7 %collective-permute-start.8 = (bf16[512,512]{1,0:T(8,128)(2,1)S(1)}, bf16[512,512]{1,0:T(8,128)(2,1)S(1)}, u32[]{:S(2)}, u32[]{:S(2)}) collective-permute-start(bf16[512,512]{1,0:T(8,128)(2,1)S(1)} %maximum_select_fusion.1), channel_id=1, source_target_pairs={{0,16},{1,17},{2,18},{3,19},{4,20},{5,21},{6,22},{7,23},{8,24},{9,... | collective-permute-start | bytes 1572872 | tf_op jit(solution)/shard_map/ppermute | solution.py:14
  262.8 21.5 %copy-start.14 = (bf16[512,512]{1,0:T(8,128)(2,1)S(1)}, bf16[512,512]{1,0:T(8,128)(2,1)}, u32[]{:S(2)}) copy-start(bf16[512,512]{1,0:T(8,128)(2,1)} %param.21) | copy-start | bytes 1572868
  335.5 5.0 %copy-start.15 = (bf16[512,512]{1,0:T(8,128)(2,1)S(1)}, bf16[512,512]{1,0:T(8,128)(2,1)}, u32[]{:S(2)}) copy-start(bf16[512,512]{1,0:T(8,128)(2,1)} %param.22) | copy-start | bytes 1572868
  351.1 10.2 %slice-start = ((s8[8388608]{0:T(1024)(128)(4,1)}), s8[4194304]{0:T(1024)(128)(4,1)S(1)}, s32[]{:S(2)}) async-start(s8[8388608]{0:T(1024)(128)(4,1)} %bitcast.72), calls=%async_computation.3 | async-start | bytes 8388608
  356.2 5.1 %slice-start.1 = ((s8[8388608]{0:T(1024)(128)(4,1)}), s8[4194304]{0:T(1024)(128)(4,1)S(1)}, s32[]{:S(2)}) async-start(s8[8388608]{0:T(1024)(128)(4,1)} %bitcast.72), calls=%async_computation.4 | async-start | bytes 8388608
  366.0 1.6 copy-start.5
  366.0 1.7 copy-start.7
  366.0 5.0 %copy-start.1 = (bf16[512,512]{1,0:T(8,128)(2,1)S(1)}, bf16[512,512]{1,0:T(8,128)(2,1)}, u32[]{:S(2)}) copy-start(bf16[512,512]{1,0:T(8,128)(2,1)} %param.17) | copy-start | bytes 1572868
